TPU v7x, 32 devices: a whole 2x2x4 slice. The times are simulated.
32 devices in a mesh: kgrp: 4 (over x, core), row: 4 (over z), col: 2 (over y).
Axes of the slice: x: 2, y: 2, z: 4, core: 2. Of those that a mesh axis runs over, the one named last changes fastest.
Arguments:
- occ_orbitals: bfloat16 [8, 1024, 2, 512], P('kgrp', ('row', 'col')), may hold values from -5 to 5
- emp_orbitals: bfloat16 [8, 1024, 2, 512], P('kgrp', ('row', 'col')), may hold values from -5 to 5
- energies: float32 [2, 8, 512], replicated, may hold values from 0.05 to 1.5
- band_order: int32 [2, 8, 512], replicated, may hold values from 0 to 511, each once within a row
- imag_times: float32 [2], replicated, may hold values from 0.3 to 3
- kq_map: int32 [2, 8], replicated, may hold values from 0 to 7, each once within a row
- slot_kpoint: int32 [8], replicated, may hold values from 0 to 7, each once
Outputs:
- suscept: float32 [2, 2, 2, 512, 2, 1024], P(None, None, 'col', 'kgrp', None, 'row')
Inputs may be any that keep to these rules, and one draw needn't show every extreme that they name: `kq_map`: each row is a permutation of the k-point ids. `slot_kpoint`: a permutation of the k-point ids. `band_order`: each row over the last dimension is a permutation of the ranks.
All inputs are finite; a program needn't handle non-finite values.
Results may differ from a plain program's by a relative error of at most 0.0003.
Values may be sent and summed in bfloat16 or wider, within the bound.
No kernel may reach another device: no remote copies, remote signals or barrier semaphores. Data moves between devices by JAX's collectives and lax.ppermute only.
A program may use at most 64 MiB of HBM per device.

v0:
```python
import jax
import jax.numpy as jnp
from jax import lax
from jax.sharding import PartitionSpec as P


def table_row(lookup_table, wanted):
    positions = jnp.arange(lookup_table.shape[0], dtype=jnp.int32)
    chosen = positions[:, None] == wanted
    return jnp.sum(jnp.where(chosen, lookup_table, jnp.zeros_like(lookup_table)), axis=0)


def band_weights(levels, band_rank, imag_times):
    picked = jnp.take(levels, band_rank, axis=0)
    return jnp.exp(-picked[None, :] * imag_times[:, None])


def green_tile(row_panel, col_panel, weights):
    times_count = weights.shape[0]
    scaled = (row_panel[None] * weights[:, None, None, :]).astype(jnp.bfloat16)
    scaled = scaled.reshape(times_count, row_panel.shape[0], -1)
    turned = jnp.concatenate([-col_panel[:, 1], col_panel[:, 0]], axis=1)
    stacked = jnp.concatenate([col_panel.reshape(col_panel.shape[0], -1), turned], axis=0)
    result = lax.dot_general(
        stacked, scaled, (((1,), (2,)), ((), ())), preferred_element_type=jnp.float32
    )
    return result.reshape(2, col_panel.shape[0], times_count, row_panel.shape[0])


def pair_term(held_tile, moved_tile, factor):
    real_part = held_tile[0] * moved_tile[0] + held_tile[1] * moved_tile[1]
    imag_part = held_tile[1] * moved_tile[0] - held_tile[0] * moved_tile[1]
    return factor * jnp.stack([real_part, imag_part])


def source_slots(kq_map, slot_kpoint, own_slots):
    positions = jnp.arange(slot_kpoint.shape[0], dtype=jnp.int32)
    own_kpoint = jnp.sum(
        jnp.where(own_slots[:, None] == positions[None, :], slot_kpoint[None, :], 0), axis=1
    )
    target = jnp.sum(
        jnp.where(own_kpoint[None, :, None] == positions[None, None, :], kq_map[:, None, :], 0),
        axis=2,
    )
    return jnp.sum(
        jnp.where(target[:, :, None] == slot_kpoint[None, None, :], positions[None, None, :], 0),
        axis=2,
    )


def shards(occ_orbitals, emp_orbitals, energies, band_order, imag_times, kq_map, slot_kpoint):
    groups = lax.axis_size("kgrp")
    per_group = occ_orbitals.shape[0]
    kpoints = groups * per_group
    transfers = kq_map.shape[0]
    factor = -1.0 / kpoints
    own_slots = lax.axis_index("kgrp") * per_group + jnp.arange(per_group, dtype=jnp.int32)
    sources = source_slots(kq_map, slot_kpoint, own_slots)
    flat_sources = sources.reshape(-1)
    initial = jnp.zeros((flat_sources.shape[0],) + emp_orbitals.shape[1:], jnp.float32)
    block_part = lax.all_gather(emp_orbitals, "kgrp", axis=0, tiled=True)
    numbered = block_part.shape[0]
    matches = (flat_sources[:, None] == jnp.arange(numbered, dtype=jnp.int32)[None, :]).astype(
        jnp.bfloat16
    )
    update = jnp.dot(matches, block_part.reshape(numbered, -1), preferred_element_type=jnp.float32)
    fetched = update.reshape(initial.shape).astype(jnp.bfloat16)
    occ_rows, emp_rows = (
        lax.all_gather(occ_orbitals, "col", axis=1, tiled=True),
        lax.all_gather(fetched, "col", axis=1, tiled=True),
    )
    occ_cols, emp_cols = (
        lax.all_gather(occ_orbitals, "row", axis=1, tiled=True),
        lax.all_gather(fetched, "row", axis=1, tiled=True),
    )
    tiles = []
    for position in range(per_group):
        weights = band_weights(
            table_row(energies[0], own_slots[position]),
            table_row(band_order[0], own_slots[position]),
            imag_times,
        )
        tiles.append(green_tile(occ_rows[position], occ_cols[position], weights))

    def transfer_terms(transfer):
        partial_value = None
        for position in range(per_group):
            source = sources[transfer, position]
            weights = band_weights(
                table_row(energies[1], source), table_row(band_order[1], source), imag_times
            )
            moved_index = transfer * per_group + position
            moved_tile = green_tile(emp_rows[moved_index], emp_cols[moved_index], weights)
            addition = pair_term(tiles[position], moved_tile, factor)
            partial_value = addition if partial_value is None else partial_value + addition
        return partial_value

    terms_all = jnp.stack([transfer_terms(transfer) for transfer in range(transfers)], axis=1)
    summed = lax.psum_scatter(terms_all, "kgrp", scatter_dimension=2, tiled=True)
    return summed[:, :, None]


def solution(mesh):
    in_specs = (
        P("kgrp", ("row", "col"), None, None),
        P("kgrp", ("row", "col"), None, None),
        P(),
        P(),
        P(),
        P(),
        P(),
    )
    out_specs = P(None, None, "col", "kgrp", None, "row")
    return jax.shard_map(shards, mesh=mesh, in_specs=in_specs, out_specs=out_specs, check_vma=False)
```

profile of v0, /device:TPU:0, one launch (start us, length us, event | category | flops | bytes accessed | tf_op | source)
XLA Modules:
  0.0 337.4 jit_solution(6772064076191064861)
XLA Ops:
  11.0 23.2 %all-gather.10.cloned.1.call-done = bf16[8,128,2,512]{3,1,2,0:T(8,128)(2,1)} async-done(((bf16[2,128,2,512]{3,1,2,0:T(8,128)(2,1)}), bf16[8,128,2,512]{3,1,2,0:T(8,128)(2,1)}) %all-gather.10.cloned.1.call-update) | async-done | bytes 2097168 | tf_op jit(solution)/shard_map/all_gather | solution.py:61
  34.2 5.1 %copy.75 = bf16[8,128,2,512]{3,2,1,0:T(2,128)(2,1)} copy(bf16[8,128,2,512]{3,1,2,0:T(8,128)(2,1)} %all-gather.10.cloned.1.call-done) | data formatting | bytes 4194304 | tf_op jit(solution)/shard_map/all_gather | solution.py:61
  39.3 3.2 reshape.401
  49.9 3.5 %gather_fusion = f32[512]{0:T(512)S(1)} fusion(f32[512]{0:T(512)S(1)} %get-tuple-element.21, s32[1024]{0:T(1024)S(1)} %pad_clamp_fusion.5), kind=kCustom, calls=%fused_computation.clone | custom fusion | bytes 6144 | tf_op jit(solution)/shard_map/jit(_take)/gather | solution.py:14
  53.4 3.5 %gather_fusion.1 = f32[512]{0:T(512)S(1)} fusion(f32[512]{0:T(512)S(1)} %get-tuple-element.20, s32[1024]{0:T(1024)S(1)} %pad_clamp_fusion.4), kind=kCustom, calls=%fused_computation.1.clone | custom fusion | bytes 6144 | tf_op jit(solution)/shard_map/jit(_take)/gather | solution.py:14
  56.9 3.5 %gather_fusion.2 = f32[512]{0:T(512)S(1)} fusion(f32[512]{0:T(512)S(1)} %get-tuple-element.19, s32[1024]{0:T(1024)S(1)} %pad_clamp_fusion.3), kind=kCustom, calls=%fused_computation.2.clone | custom fusion | bytes 6144 | tf_op jit(solution)/shard_map/jit(_take)/gather | solution.py:14
  60.5 3.5 %gather_fusion.4 = f32[512]{0:T(512)S(1)} fusion(f32[512]{0:T(512)S(1)} %get-tuple-element.18, s32[1024]{0:T(1024)S(1)} %pad_clamp_fusion.1), kind=kCustom, calls=%fused_computation.4.clone | custom fusion | bytes 6144 | tf_op jit(solution)/shard_map/jit(_take)/gather | solution.py:14
  64.0 3.5 %gather_fusion.3 = f32[512]{0:T(512)S(1)} fusion(f32[512]{0:T(512)S(1)} %get-tuple-element.16, s32[1024]{0:T(1024)S(1)} %pad_clamp_fusion.2), kind=kCustom, calls=%fused_computation.3.clone | custom fusion | bytes 6144 | tf_op jit(solution)/shard_map/jit(_take)/gather | solution.py:14
  67.5 3.5 %gather_fusion.5 = f32[512]{0:T(512)S(1)} fusion(f32[512]{0:T(512)S(1)} %get-tuple-element.17, s32[1024]{0:T(1024)S(1)} %pad_clamp_fusion), kind=kCustom, calls=%fused_computation.5.clone | custom fusion | bytes 6144 | tf_op jit(solution)/shard_map/jit(_take)/gather | solution.py:14
  75.7 28.6 %all-gather.6.cloned.1.call-done = bf16[2,512,2,512]{3,1,2,0:T(8,128)(2,1)} async-done(((bf16[2,128,2,512]{3,1,2,0:T(8,128)(2,1)}), bf16[2,512,2,512]{3,1,2,0:T(8,128)(2,1)}) %all-gather.6.cloned.1.call-update) | async-done | bytes 2097168 | tf_op jit(solution)/shard_map/all_gather | solution.py:73
  104.3 3.3 fusion.78
  116.0 2.6 fusion.11
  118.6 19.1 %all-gather.14.cloned.1.call-done = bf16[4,256,2,512]{3,0,2,1:T(4,128)(2,1)} async-done(((bf16[4,128,2,512]{3,0,2,1:T(4,128)(2,1)}), bf16[4,256,2,512]{3,0,2,1:T(4,128)(2,1)}) %all-gather.14.cloned.1.call-update) | async-done | bytes 2097168 | tf_op jit(solution)/shard_map/all_gather | solution.py:70
  137.7 18.5 %fusion.34 = (f32[256,2,512]{2,1,0:T(2,128)S(1)}, f32[256,2,512]{2,1,0:T(2,128)S(1)}, f32[256,2,512]{2,1,0:T(2,128)S(1)}, f32[256,2,512]{2,1,0:T(2,128)S(1)}) fusion(bf16[4,256,2,512]{3,0,2,1:T(4,128)(2,1)} %all-gather.14.cloned.1.call-done), kind=kLoop, calls=%fused_computation.59 | loop fusion | flops 1048576 | bytes 6291456 | tf_op jit(solution)/shard_map/mul | solution.py:20
  160.9 59.0 %all-gather.12.cloned.1.call-done = bf16[4,512,2,512]{3,0,2,1:T(4,128)(2,1)} async-done(((bf16[4,128,2,512]{3,0,2,1:T(4,128)(2,1)}), bf16[4,512,2,512]{3,0,2,1:T(4,128)(2,1)}) %all-gather.12.cloned.1.call-update) | async-done | bytes 4194320 | tf_op jit(solution)/shard_map/all_gather | solution.py:74
  219.9 14.6 %fusion.77 = (bf16[1,512,2,512]{3,0,2,1:T(2,128)(2,1)}, bf16[1,512,2,512]{3,0,2,1:T(2,128)(2,1)}, bf16[1,512,2,512]{3,0,2,1:T(2,128)(2,1)}, bf16[1,512,2,512]{3,0,2,1:T(2,128)(2,1)S(1)}) fusion(bf16[4,512,2,512]{3,0,2,1:T(4,128)(2,1)} %all-gather.12.cloned.1.call-done), kind=kLoop, calls=%fused_computation.184 | loop fusion | bytes 8388608 | tf_op jit(solution)/shard_map/slice | solution.py:93
  234.5 5.8 %copy.93 = bf16[1,512,2,512]{1,3,2,0:T(8,128)(2,1)} copy(bf16[1,512,2,512]{3,0,2,1:T(2,128)(2,1)} %get-tuple-element.24) | data formatting | bytes 2097152
  240.3 4.2 %copy_bitcast_fusion.2 = (bf16[512,2,512]{2,0,1:T(8,128)(2,1)}, bf16[512,2,512]{2,0,1:T(8,128)(2,1)}) fusion(bf16[1,512,2,512]{3,0,2,1:T(2,128)(2,1)} %get-tuple-element.24, bf16[1,512,2,512]{3,0,2,1:T(2,128)(2,1)} %get-tuple-element.26), kind=kLoop, calls=%fused_computation.64 | loop fusion | bytes 4194304 | tf_op jit(solution)/shard_map/squeeze | solution.py:93
  244.5 5.8 %copy.92 = bf16[1,512,2,512]{1,3,2,0:T(8,128)(2,1)} copy(bf16[1,512,2,512]{3,0,2,1:T(2,128)(2,1)} %get-tuple-element.26) | data formatting | bytes 2097152
  250.3 4.8 %copy.94 = bf16[1,512,2,512]{1,3,2,0:T(8,128)(2,1)S(1)} copy(bf16[1,512,2,512]{3,0,2,1:T(2,128)(2,1)} %get-tuple-element.25) | data formatting | bytes 2097152
  255.2 3.6 %copy_bitcast_fusion = (bf16[512,2,512]{2,0,1:T(8,128)(2,1)}, bf16[512,2,512]{2,0,1:T(8,128)(2,1)}) fusion(bf16[1,512,2,512]{3,0,2,1:T(2,128)(2,1)S(1)} %get-tuple-element.27, bf16[1,512,2,512]{3,0,2,1:T(2,128)(2,1)} %get-tuple-element.25), kind=kLoop, calls=%fused_computation.62 | loop fusion | bytes 4194304 | tf_op jit(solution)/shard_map/squeeze | solution.py:93
  258.7 4.2 %copy.95 = bf16[1,512,2,512]{1,3,2,0:T(8,128)(2,1)} copy(bf16[1,512,2,512]{3,0,2,1:T(2,128)(2,1)S(1)} %get-tuple-element.27) | data formatting | bytes 2097152
  284.4 43.2 %reduce-scatter.2.cloned.1.call-done = f32[2,2,128,2,256]{4,2,3,1,0:T(8,128)} async-done(((f32[2,2,512,2,256]{4,2,3,1,0:T(8,128)}), f32[2,2,128,2,256]{4,2,3,1,0:T(8,128)}) %reduce-scatter.2.cloned.1.call-update) | async-done | bytes 1048592 | tf_op jit(solution)/shard_map/reduce_scatter | solution.py:99
  327.6 3.0 copy.90
  (150 shorter events, 50.6 us)
Async XLA Ops:
  6.5 2.8 copy-start.10
  6.5 3.8 %copy-start.29 = (s32[8]{0:T(128)S(1)}, s32[8]{0:T(128)}, u32[]{:S(2)}) copy-start(s32[8]{0:T(128)} %param.15) | copy-start | bytes 100
  6.5 4.0 %copy-start.27 = (s32[2,8]{1,0:T(2,128)S(1)}, s32[2,8]{1,0:T(2,128)}, u32[]{:S(2)}) copy-start(s32[2,8]{1,0:T(2,128)} %param.14) | copy-start | bytes 196
  6.5 27.7 %all-gather.10.cloned.1.call-start = ((), (), s32[]{:S(2)}) async-start(), calls=%async_computation.3 | async-start | bytes 2621440 | tf_op jit(solution)/shard_map/all_gather | solution.py:61
  8.5 62.9 %all-gather.8.cloned.1.call-start = ((), (), s32[]{:S(2)}) async-start(), calls=%async_computation.2 | async-start | bytes 1572864 | tf_op jit(solution)/shard_map/all_gather | solution.py:69
  9.3 95.1 %all-gather.6.cloned.1.call-start = ((), (), s32[]{:S(2)}) async-start(), calls=%async_computation.1 | async-start | bytes 2621440 | tf_op jit(solution)/shard_map/all_gather | solution.py:73
  10.2 127.4 %all-gather.14.cloned.1.call-start = ((), (), s32[]{:S(2)}) async-start(), calls=%async_computation.5 | async-start | bytes 3145728 | tf_op jit(solution)/shard_map/all_gather | solution.py:70
  42.5 6.9 %copy-start.25 = (s32[2,8,512]{2,1,0:T(8,128)S(1)}, s32[2,8,512]{2,1,0:T(8,128)}, u32[]{:S(2)}) copy-start(s32[2,8,512]{2,1,0:T(8,128)} %param.12) | copy-start | bytes 98308
  42.5 7.1 %copy-start.26 = (f32[2,8,512]{2,1,0:T(8,128)S(1)}, f32[2,8,512]{2,1,0:T(8,128)}, u32[]{:S(2)}) copy-start(f32[2,8,512]{2,1,0:T(8,128)} %param.11) | copy-start | bytes 98308
  44.2 175.6 %all-gather.12.cloned.1.call-start = ((), (), s32[]{:S(2)}) async-start(), calls=%async_computation.4 | async-start | bytes 5242880 | tf_op jit(solution)/shard_map/all_gather | solution.py:74
  49.7 277.9 %reduce-scatter.2.cloned.1.call-start = ((), (), s32[]{:S(2)}) async-start(), calls=%async_computation.6 | async-start | bytes 5242880 | tf_op jit(solution)/shard_map/reduce_scatter | solution.py:99
  64.0 7.1 %copy-start.28 = (f32[2]{0:T(128)S(1)}, f32[2]{0:T(128)}, u32[]{:S(2)}) copy-start(f32[2]{0:T(128)} %param.13) | copy-start | bytes 28
  109.5 1.9 copy-start.6
  111.6 1.7 copy-start.22
  113.3 2.6 copy-start.17
  113.3 2.6 copy-start.21
  262.9 2.5 copy-start
  262.9 3.8 %copy-start.4 = (bf16[512,2,512]{2,0,1:T(8,128)(2,1)S(1)}, bf16[512,2,512]{2,0,1:T(8,128)(2,1)}, u32[]{:S(2)}) copy-start(bf16[512,2,512]{2,0,1:T(8,128)(2,1)} %get-tuple-element.70) | copy-start | bytes 3145732
  266.7 2.4 copy-start.1
  269.1 1.9 copy-start.3
  271.0 1.6 copy-start.19
  271.0 1.7 copy-start.23
  271.0 1.9 copy-start.24
  274.4 1.6 copy-start.9
  (12 other events, 16.8 us)
Sparse Core Ops, SparseCore 0:
  8.9 25.2 all-gather.9
  35.8 21.2 all-gather.7
  58.7 45.6 all-gather.5
  105.7 31.8 all-gather.13
  139.1 80.7 all-gather.11
  284.5 43.0 reduce-scatter.1
where the time goes:
time: 338 us; the launch traced here: 337 us
  waiting for transfers between devices  174 us (51%)
  local copies, waits for them, and re-layouts  106 us (31%)
  other arithmetic  30.8 us (9%)
  between operations  14 us (4%)
  matrix products  12.1 us (4%)
    all_gather x1, waiting for transfers between devices, shards(): lax.all_gather(fetched, 'row', axis=1, tiled=True)  59 us
    reduce_scatter x1, waiting for transfers between devices, shards(): lax.psum_scatter(terms_all, 'kgrp', scatter_dimension=2, tiled=True)  43.2 us
    unnamed x84, local copies, waits for them, and re-layouts  36.8 us
    all_gather x1, waiting for transfers between devices, shards(): lax.all_gather(occ_orbitals, 'row', axis=1, tiled=True)  28.6 us
    all_gather x1, waiting for transfers between devices, shards(): block_part = lax.all_gather(emp_orbitals, 'kgrp', axis=0, tiled=True)  23.2 us
    gather x6, local copies, waits for them, and re-layouts, band_weights(): picked = jnp.take(levels, band_rank, axis=0)  20.9 us
    mul x2, other arithmetic, green_tile(): scaled = (row_panel[None] * weights[:, None, None, :]).astype(jnp.bfloat16)  20.4 us
    all_gather x1, waiting for transfers between devices, shards(): lax.all_gather(fetched, 'col', axis=1, tiled=True)  19.1 us
  transfers between devices with their start and end apart: 6, of which 5 were waited for; matrix products, arithmetic and copies ran while one was open for 23% of the time, Pallas kernels for 0%

commit v1 on v0

--- a/solution.py
+++ b/solution.py
@@ -2,6 +2,12 @@
 import jax.numpy as jnp
 from jax import lax
 from jax.sharding import PartitionSpec as P
+
+
+def gathered_along(block, name, d):
+    parts = lax.all_gather(block, name, axis=0, tiled=False)
+    whole = jnp.concatenate(parts, axis=d)
+    return whole
 
 
 def table_row(lookup_table, wanted):
@@ -71,7 +77,7 @@
     )
     occ_cols, emp_cols = (
         lax.all_gather(occ_orbitals, "row", axis=1, tiled=True),
-        lax.all_gather(fetched, "row", axis=1, tiled=True),
+        gathered_along(fetched, "row", 1),
     )
     tiles = []
     for position in range(per_group):

time: 338 us -> 294 us (0.87)
  local copies, waits for them, and re-layouts: 106 us -> 64.2 us
    unnamed x84 -> x56, local copies, waits for them, and re-layouts: 36.8 us -> 13.7 us
    slice x1 -> x5, local copies, waits for them, and re-layouts: 14.6 us -> 4.78 us  [transfer_terms(): emp_cols[moved_index]]
    squeeze x2 -> x0, local copies, waits for them, and re-layouts: 7.79 us -> none  [transfer_terms(): emp_cols[moved_index]]
    another operation x6 -> x2, local copies, waits for them, and re-layouts: 9 us -> 2.67 us  [green_tile(): col_panel.reshape(col_panel.shape[0], -1)]
  transfers between devices with their start and end apart: 6 -> 6, of which waited for: 5 -> 5; matrix products, arithmetic and copies ran while one was open for 23% -> 27% of each run, Pallas kernels for 0% -> 0%
where the time goes in v1:
time: 294 us; the launch traced here: 293 us
  waiting for transfers between devices  173 us (59%)
  local copies, waits for them, and re-layouts  64.2 us (22%)
  other arithmetic  29.7 us (10%)
  between operations  14.1 us (5%)
  matrix products  11.1 us (4%)
    all_gather x1, waiting for transfers between devices, gathered_along(): parts = lax.all_gather(block, name, axis=0, tiled=False)  59.9 us
    reduce_scatter x1, waiting for transfers between devices, shards(): lax.psum_scatter(terms_all, 'kgrp', scatter_dimension=2, tiled=True)  43.2 us
    all_gather x1, waiting for transfers between devices, shards(): lax.all_gather(occ_orbitals, 'row', axis=1, tiled=True)  25.9 us
    all_gather x1, waiting for transfers between devices, shards(): block_part = lax.all_gather(emp_orbitals, 'kgrp', axis=0, tiled=True)  23.2 us
    gather x6, local copies, waits for them, and re-layouts, band_weights(): picked = jnp.take(levels, band_rank, axis=0)  20.9 us
    all_gather x1, waiting for transfers between devices, shards(): lax.all_gather(fetched, 'col', axis=1, tiled=True)  20.4 us
    mul x2, other arithmetic, green_tile(): scaled = (row_panel[None] * weights[:, None, None, :]).astype(jnp.bfloat16)  20.4 us
    unnamed x56, local copies, waits for them, and re-layouts  13.7 us
  transfers between devices with their start and end apart: 6, of which 5 were waited for; matrix products, arithmetic and copies ran while one was open for 27% of the time, Pallas kernels for 0%

profile of v1, /device:TPU:0, one launch (start us, length us, event | category | flops | bytes accessed | tf_op | source)
XLA Modules:
  0.0 292.9 jit_solution(9556126760362079939)
XLA Ops:
  6.5 1.9 copy.62
  11.0 23.2 %all-gather.11.cloned.1.call-done = bf16[8,128,2,512]{3,1,2,0:T(8,128)(2,1)} async-done(((bf16[2,128,2,512]{3,1,2,0:T(8,128)(2,1)}), bf16[8,128,2,512]{3,1,2,0:T(8,128)(2,1)}) %all-gather.11.cloned.1.call-update) | async-done | bytes 2097168 | tf_op jit(solution)/shard_map/all_gather | solution.py:67
  34.2 5.0 %copy.63 = bf16[8,128,2,512]{3,2,1,0:T(2,128)(2,1)} copy(bf16[8,128,2,512]{3,1,2,0:T(8,128)(2,1)} %all-gather.11.cloned.1.call-done) | data formatting | bytes 4194304 | tf_op jit(solution)/shard_map/all_gather | solution.py:67
  39.3 3.2 %reshape.417 = bf16[8,131072]{1,0:T(8,128)(2,1)S(1)} reshape(bf16[8,128,2,512]{3,2,1,0:T(2,128)(2,1)} %copy.63) | data formatting | bytes 4194304 | tf_op jit(solution)/shard_map/reshape | solution.py:72
  42.5 1.7 convolution_convert_fusion
  49.8 2.5 copy.64
  52.6 3.5 %gather_fusion.5 = f32[512]{0:T(512)S(1)} fusion(f32[512]{0:T(512)S(1)} %get-tuple-element.17, s32[1024]{0:T(1024)S(1)} %pad_clamp_fusion), kind=kCustom, calls=%fused_computation.5.clone | custom fusion | bytes 6144 | tf_op jit(solution)/shard_map/jit(_take)/gather | solution.py:20
  56.1 3.5 %gather_fusion.4 = f32[512]{0:T(512)S(1)} fusion(f32[512]{0:T(512)S(1)} %get-tuple-element.18, s32[1024]{0:T(1024)S(1)} %pad_clamp_fusion.1), kind=kCustom, calls=%fused_computation.4.clone | custom fusion | bytes 6144 | tf_op jit(solution)/shard_map/jit(_take)/gather | solution.py:20
  59.6 3.5 %gather_fusion.3 = f32[512]{0:T(512)S(1)} fusion(f32[512]{0:T(512)S(1)} %get-tuple-element.16, s32[1024]{0:T(1024)S(1)} %pad_clamp_fusion.2), kind=kCustom, calls=%fused_computation.3.clone | custom fusion | bytes 6144 | tf_op jit(solution)/shard_map/jit(_take)/gather | solution.py:20
  63.1 3.5 %gather_fusion.2 = f32[512]{0:T(512)S(1)} fusion(f32[512]{0:T(512)S(1)} %get-tuple-element.19, s32[1024]{0:T(1024)S(1)} %pad_clamp_fusion.3), kind=kCustom, calls=%fused_computation.2.clone | custom fusion | bytes 6144 | tf_op jit(solution)/shard_map/jit(_take)/gather | solution.py:20
  66.7 3.5 %gather_fusion.1 = f32[512]{0:T(512)S(1)} fusion(f32[512]{0:T(512)S(1)} %get-tuple-element.20, s32[1024]{0:T(1024)S(1)} %pad_clamp_fusion.4), kind=kCustom, calls=%fused_computation.1.clone | custom fusion | bytes 6144 | tf_op jit(solution)/shard_map/jit(_take)/gather | solution.py:20
  70.2 3.5 %gather_fusion = f32[512]{0:T(512)S(1)} fusion(f32[512]{0:T(512)S(1)} %get-tuple-element.21, s32[1024]{0:T(1024)S(1)} %pad_clamp_fusion.5), kind=kCustom, calls=%fused_computation.clone | custom fusion | bytes 6144 | tf_op jit(solution)/shard_map/jit(_take)/gather | solution.py:20
  74.1 1.9 slice_convert_fusion.4
  78.4 25.9 %all-gather.7.cloned.1.call-done = bf16[2,512,2,512]{3,1,2,0:T(8,128)(2,1)} async-done(((bf16[2,128,2,512]{3,1,2,0:T(8,128)(2,1)}), bf16[2,512,2,512]{3,1,2,0:T(8,128)(2,1)}) %all-gather.7.cloned.1.call-update) | async-done | bytes 2097168 | tf_op jit(solution)/shard_map/all_gather | solution.py:79
  104.3 3.3 %fusion.78 = (bf16[1,512,2,512]{3,1,2,0:T(8,128)(2,1)S(1)}, bf16[512,2,512]{2,0,1:T(8,128)(2,1)}, bf16[512,2,512]{2,0,1:T(8,128)(2,1)}, bf16[1,512,2,512]{3,1,2,0:T(8,128)(2,1)S(1)}) fusion(bf16[2,512,2,512]{3,1,2,0:T(8,128)(2,1)} %all-gather.7.cloned.1.call-done), kind=kLoop, calls=%fused_computation.182 | loop fusion | bytes 6291456 | tf_op jit(solution)/shard_map/slice | solution.py:89
  113.3 2.6 fusion.11
  117.2 20.4 %all-gather.13.cloned.1.call-done = bf16[4,256,2,512]{3,0,2,1:T(4,128)(2,1)} async-done(((bf16[4,128,2,512]{3,0,2,1:T(4,128)(2,1)}), bf16[4,256,2,512]{3,0,2,1:T(4,128)(2,1)}) %all-gather.13.cloned.1.call-update) | async-done | bytes 2097168 | tf_op jit(solution)/shard_map/all_gather | solution.py:76
  137.7 18.5 %fusion.34 = (f32[256,2,512]{2,1,0:T(2,128)S(1)}, f32[256,2,512]{2,1,0:T(2,128)S(1)}, f32[256,2,512]{2,1,0:T(2,128)S(1)}, f32[256,2,512]{2,1,0:T(2,128)S(1)}) fusion(bf16[4,256,2,512]{3,0,2,1:T(4,128)(2,1)} %all-gather.13.cloned.1.call-done), kind=kLoop, calls=%fused_computation.60 | loop fusion | flops 1048576 | bytes 6291456 | tf_op jit(solution)/shard_map/mul | solution.py:26
  160.0 59.9 %all-gather.15.cloned.1.call-done = bf16[16,128,2,512]{3,1,2,0:T(8,128)(2,1)} async-done(((bf16[4,128,2,512]{3,1,2,0:T(8,128)(2,1)}), bf16[16,128,2,512]{3,1,2,0:T(8,128)(2,1)}) %all-gather.15.cloned.1.call-update) | async-done | bytes 4194320 | tf_op jit(solution)/shard_map/all_gather | solution.py:8
  219.9 2.6 copy.91
  234.9 1.6 fusion.5
  237.6 2.3 pad_maximum_fusion
  239.9 43.2 %reduce-scatter.2.cloned.1.call-done = f32[2,2,128,2,256]{4,2,3,1,0:T(8,128)} async-done(((f32[2,2,512,2,256]{4,2,3,1,0:T(8,128)}), f32[2,2,128,2,256]{4,2,3,1,0:T(8,128)}) %reduce-scatter.2.cloned.1.call-update) | async-done | bytes 1048592 | tf_op jit(solution)/shard_map/reduce_scatter | solution.py:105
  283.1 3.0 %copy.72 = f32[2,2,1,128,2,256]{5,4,3,2,1,0:T(2,128)} copy(f32[2,2,1,128,2,256]{5,3,4,1,0,2:T(8,128)} %bitcast.201) | data formatting | bytes 2097152 | tf_op jit(solution)/shard_map/broadcast_in_dim | solution.py:106
  (122 shorter events, 35.0 us)
Async XLA Ops:
  6.5 2.8 copy-start.3
  6.5 3.7 %copy-start.15 = (s32[8]{0:T(128)S(1)}, s32[8]{0:T(128)}, u32[]{:S(2)}) copy-start(s32[8]{0:T(128)} %param.15) | copy-start | bytes 100
  6.5 4.0 %copy-start.13 = (s32[2,8]{1,0:T(2,128)S(1)}, s32[2,8]{1,0:T(2,128)}, u32[]{:S(2)}) copy-start(s32[2,8]{1,0:T(2,128)} %param.14) | copy-start | bytes 196
  6.5 27.7 %all-gather.11.cloned.1.call-start = ((), (), s32[]{:S(2)}) async-start(), calls=%async_computation.3 | async-start | bytes 2621440 | tf_op jit(solution)/shard_map/all_gather | solution.py:67
  8.5 65.6 %all-gather.9.cloned.1.call-start = ((), (), s32[]{:S(2)}) async-start(), calls=%async_computation.2 | async-start | bytes 1572864 | tf_op jit(solution)/shard_map/all_gather | solution.py:75
  9.3 95.1 %all-gather.7.cloned.1.call-start = ((), (), s32[]{:S(2)}) async-start(), calls=%async_computation.1 | async-start | bytes 2621440 | tf_op jit(solution)/shard_map/all_gather | solution.py:79
  10.2 127.5 %all-gather.13.cloned.1.call-start = ((), (), s32[]{:S(2)}) async-start(), calls=%async_computation.4 | async-start | bytes 3145728 | tf_op jit(solution)/shard_map/all_gather | solution.py:76
  42.4 7.1 %copy-start.11 = (s32[2,8,512]{2,1,0:T(8,128)S(1)}, s32[2,8,512]{2,1,0:T(8,128)}, u32[]{:S(2)}) copy-start(s32[2,8,512]{2,1,0:T(8,128)} %param.12) | copy-start | bytes 98308
  42.4 7.3 %copy-start.12 = (f32[2,8,512]{2,1,0:T(8,128)S(1)}, f32[2,8,512]{2,1,0:T(8,128)}, u32[]{:S(2)}) copy-start(f32[2,8,512]{2,1,0:T(8,128)} %param.11) | copy-start | bytes 98308
  44.2 175.6 %all-gather.15.cloned.1.call-start = ((), (), s32[]{:S(2)}) async-start(), calls=%async_computation.6 | async-start | bytes 5242880 | tf_op jit(solution)/shard_map/all_gather | solution.py:8
  52.4 230.7 %reduce-scatter.2.cloned.1.call-start = ((), (), s32[]{:S(2)}) async-start(), calls=%async_computation.5 | async-start | bytes 5242880 | tf_op jit(solution)/shard_map/reduce_scatter | solution.py:105
  66.7 7.1 %copy-start.14 = (f32[2]{0:T(128)S(1)}, f32[2]{0:T(128)}, u32[]{:S(2)}) copy-start(f32[2]{0:T(128)} %param.13) | copy-start | bytes 28
  109.5 1.9 copy-start
  110.1 1.6 copy-start.1
  111.6 1.3 copy-start.8
  111.6 1.7 copy-start.10
  113.3 2.6 copy-start.7
  113.3 2.6 copy-start.9
  228.3 1.2 copy-start.6
  229.5 1.3 copy-start.5
  230.8 1.6 copy-start.2
  232.4 1.2 copy-start.4
Sparse Core Ops, SparseCore 0:
  8.9 25.2 all-gather.10
  35.8 21.2 all-gather.8
  58.7 45.6 all-gather.6
  105.7 31.8 all-gather.12
  139.1 80.7 all-gather.14
  240.0 43.0 reduce-scatter.1
